TPU v7x, 32 devices: a whole 2x2x4 slice. The times are simulated.
32 devices in a mesh: grp: 2 (over y), basin: 4 (over z), chain: 2 (over x), mem: 2 (over core).
Axes of the slice: x: 2, y: 2, z: 4, core: 2. Of those that a mesh axis runs over, the one named last changes fastest.
Arguments:
- runoff: float32 [2, 64, 32, 2, 2048], P('mem', 'basin', 'grp', 'chain'), parts along dimension 2, may hold values from 0.002 to 0.02
- directions: int32 [32, 2, 2048], P(('grp', 'basin'), 'chain'), parts along dimension 0, may hold values from 0 to 2
Outputs:
- accumulation: float32 [128, 32, 2, 2048], P('mem', ('grp', 'basin'), 'chain'), parts along dimension 1
There are 2 independent parts, one for each index of `grp`. A program takes and returns all parts, laid end to end along the dimension named above; each array names one. Nothing has to cross between parts.
Inputs may be any that keep to these rules, and one draw needn't show every extreme that they name: `directions`: direction codes of forward three-direction routing: 0 east, 1 north-east, 2 south-east along the flow.
All inputs are finite; a program needn't handle non-finite values.
Results may differ from a plain program's by a relative error of at most 0.0003.
Values sent between devices are 32-bit elements; how exact they have to be, the bound alone decides.
No kernel may reach another device: no remote copies, remote signals or barrier semaphores. Data moves between devices by JAX's collectives and lax.ppermute only.
A program may use at most 128 MiB of HBM per device.

v0:
```python
import jax
import jax.numpy as jnp
from jax import lax
from jax.sharding import PartitionSpec as P

ROWS = 128


def from_behind(value, axis, by):
    count = lax.axis_size(axis)
    pairs = [(i, i + by) for i in range(count) if 0 <= i + by < count]
    return lax.ppermute(value, axis, pairs)


def target_rows(directions):
    cell_count = directions.shape[-1]
    row_ids = jnp.arange(cell_count, dtype=jnp.int32) % ROWS
    offsets = jnp.where(directions == 1, -1, jnp.where(directions == 2, 1, 0)).astype(jnp.int32)
    return jnp.clip(row_ids + offsets, 0, ROWS - 1)


def column_onehot(target_col, kind):
    lane_ids = jnp.arange(ROWS, dtype=jnp.int32)
    return (target_col[..., None] == lane_ids).astype(kind)


def sweep_tile(water_cols, targets, inflow):

    def advance(carried, column_data):
        water_col, target_col = column_data
        summed = water_col + carried
        passed = jnp.einsum(
            "mtj,tji->mti",
            summed,
            column_onehot(target_col, jnp.float32),
            precision=lax.Precision.HIGHEST,
        )
        return (passed, summed)

    return lax.scan(advance, inflow, (jnp.moveaxis(water_cols, 2, 0), jnp.moveaxis(targets, 1, 0)))


def section_matrix(targets):
    tile_count = targets.shape[0]
    start_map = jnp.broadcast_to(jnp.eye(ROWS, dtype=jnp.bfloat16), (tile_count, ROWS, ROWS))

    def chain_step(product, target_col):
        advanced = jnp.einsum(
            "tij,tjk->tik",
            product,
            column_onehot(target_col, jnp.bfloat16),
            preferred_element_type=jnp.float32,
        )
        return (advanced.astype(jnp.bfloat16), None)

    final_map, _ = lax.scan(chain_step, start_map, jnp.moveaxis(targets, 1, 0))
    return final_map.astype(jnp.float32)


def route_chain(water_cols, targets):
    member_count, tile_count = (water_cols.shape[0], water_cols.shape[1])
    no_inflow = jnp.zeros((member_count, tile_count, ROWS), jnp.float32)
    local_flow, _ = sweep_tile(water_cols, targets, no_inflow)
    panel_map = section_matrix(targets)

    def relay_step(counter, state):
        total_out, received = state
        received = from_behind(total_out, "chain", 1)
        total_out = local_flow + jnp.einsum(
            "mtj,tjk->mtk", received, panel_map, precision=lax.Precision.HIGHEST
        )
        return (total_out, received)

    _, inflow = lax.fori_loop(0, lax.axis_size("chain") - 1, relay_step, (local_flow, no_inflow))
    _, columns_out = sweep_tile(water_cols, targets, inflow)
    return columns_out


def local(runoff, directions):
    cell_count = runoff.shape[4]
    col_count = cell_count // ROWS
    regrouped = lax.all_to_all(runoff, "basin", split_axis=2, concat_axis=1, tiled=True)
    member_count, tile_count = (regrouped.shape[1], regrouped.shape[2])
    water_cols = regrouped.reshape(member_count, tile_count, col_count, ROWS)
    targets = target_rows(directions).reshape(tile_count, col_count, ROWS)
    columns_out = route_chain(water_cols, targets)
    return jnp.transpose(columns_out, (1, 2, 0, 3)).reshape(member_count, tile_count, 1, cell_count)


def solution(mesh):
    return jax.shard_map(
        local,
        mesh=mesh,
        in_specs=(P("mem", "basin", "grp", "chain", None), P(("grp", "basin"), "chain", None)),
        out_specs=P("mem", ("grp", "basin"), "chain", None),
        check_vma=False,
    )
```

profile of v0, /device:TPU:0, one launch (start us, length us, event | category | flops | bytes accessed | tf_op | source)
XLA Modules:
  0.0 95.5 jit_solution(6588446960508231606)
XLA Ops:
  0.0 5.1 %copy.10 = f32[1,16,16,1,2048]{4,3,1,0,2:T(1,128)} copy(f32[1,16,16,1,2048]{4,3,2,1,0:T(1,128)} %param.6) | data formatting | bytes 4194304 | tf_op args[0]
  5.1 0.0 copy-start
  5.1 6.4 %all-to-all-start = ((f32[1,16,16,1,2048]{4,3,1,0,2:T(1,128)}), f32[1,16,16,1,2048]{4,3,1,0,2:T(1,128)S(1)}, u32[]{:S(2)}, u32[]{:S(2)}) async-start(f32[1,16,16,1,2048]{4,3,1,0,2:T(1,128)} %copy.10), calls=%async_computation | async-start | bytes 4194304 | tf_op jit(solution)/shard_map/all_to_all | solution.py:82
  11.6 0.0 copy-done
  11.6 0.1 fusion.6
  11.7 48.1 %all-to-all-done = f32[1,16,16,1,2048]{4,3,1,0,2:T(1,128)S(1)} async-done(((f32[1,16,16,1,2048]{4,3,1,0,2:T(1,128)}), f32[1,16,16,1,2048]{4,3,1,0,2:T(1,128)S(1)}, u32[]{:S(2)}, u32[]{:S(2)}) %all-to-all-start) | async-done | bytes 2097184 | tf_op jit(solution)/shard_map/all_to_all | solution.py:82
  59.8 0.9 copy.17
  60.6 0.2 copy.11
  60.9 0.4 copy.18
  61.3 0.7 copy.13
  62.0 6.4 %while.4 = (s32[]{:T(128)}, f32[64,4,128]{2,0,1:T(8,128)S(1)}, s32[16,4,128]{2,1,0:T(4,128)S(1)}, f32[16,64,4,128]{3,1,2,0:T(8,128)S(1)}, s32[]{:T(128)}) while((s32[]{:T(128)}, f32[64,4,128]{2,0,1:T(8,128)S(1)}, s32[16,4,128]{2,1,0:T(4,128)S(1)}, f32[16,64,4,128]{3,1,2,0:T(8,128)S(1)}, s32[]{:T(128)}) %tuple.38), condition=%wide.region_1.2_spmd, body=%wide.region_0.1_spmd.sunk | while | flops 50429952 | bytes 661581 | solution.py:40
  62.0 0.3 convolution_bitcast_fusion.4
  62.4 0.3 convolution_bitcast_fusion.4
  62.8 0.3 convolution_bitcast_fusion.4
  63.2 0.3 convolution_bitcast_fusion.4
  63.6 0.3 convolution_bitcast_fusion.4
  64.0 0.3 convolution_bitcast_fusion.4
  64.4 0.3 convolution_bitcast_fusion.4
  64.8 0.3 convolution_bitcast_fusion.4
  65.2 0.3 convolution_bitcast_fusion.4
  65.6 0.3 convolution_bitcast_fusion.4
  66.0 0.3 convolution_bitcast_fusion.4
  66.4 0.3 convolution_bitcast_fusion.4
  66.8 0.3 convolution_bitcast_fusion.4
  67.2 0.3 convolution_bitcast_fusion.4
  67.6 0.3 convolution_bitcast_fusion.4
  68.0 0.3 convolution_bitcast_fusion.4
  68.4 3.4 %collective-permute-start = (f32[64,4,128]{2,0,1:T(8,128)S(1)}, f32[64,4,128]{2,0,1:T(8,128)S(1)}, u32[]{:S(2)}, u32[]{:S(2)}) collective-permute-start(f32[64,4,128]{2,0,1:T(8,128)S(1)} %get-tuple-element.74), channel_id=1, source_target_pairs={{0,2},{1,3},{4,6},{5,7},{8,10},{9,11},{12,14},{13,15},{16,18},{17,... | collective-permute-start | bytes 393224 | tf_op jit(solution)/shard_map/while/body/eval_jaxpr/ppermute | solution.py:12
  71.8 2.5 %collective-permute-done = f32[64,4,128]{2,0,1:T(8,128)S(1)} collective-permute-done((f32[64,4,128]{2,0,1:T(8,128)S(1)}, f32[64,4,128]{2,0,1:T(8,128)S(1)}, u32[]{:S(2)}, u32[]{:S(2)}) %collective-permute-start) | collective-permute-done | bytes 131104 | tf_op jit(solution)/shard_map/while/body/eval_jaxpr/ppermute | solution.py:12
  74.3 17.1 %while.5 = (s32[]{:T(128)}, f32[64,4,128]{2,0,1:T(8,128)S(1)}, f32[16,64,4,128]{3,1,2,0:T(8,128)}, s32[16,4,128]{2,1,0:T(4,128)S(1)}, f32[16,64,4,128]{3,1,2,0:T(8,128)S(1)}, /*index=5*/s32[]{:T(128)}) while((s32[]{:T(128)}, f32[64,4,128]{2,0,1:T(8,128)S(1)}, f32[16,64,4,128]{3,1,2,0:T(8,128)}, s32[16,4,128]{2,1,0:T(4,128)S(1)}, ...), condition=%wide.region_3.4_spmd, body=%wide.region_2.3_spmd.sunk | while | flops 50462720 | bytes 1054809 | solution.py:40
  74.3 0.7 bitcast_dynamic-update-slice_fusion.2
  75.0 0.3 convolution_bitcast_fusion.5
  75.4 0.7 bitcast_dynamic-update-slice_fusion.2
  76.1 0.3 convolution_bitcast_fusion.5
  76.5 0.7 bitcast_dynamic-update-slice_fusion.2
  77.1 0.3 convolution_bitcast_fusion.5
  77.5 0.7 bitcast_dynamic-update-slice_fusion.2
  78.2 0.3 convolution_bitcast_fusion.5
  78.6 0.7 bitcast_dynamic-update-slice_fusion.2
  79.3 0.3 convolution_bitcast_fusion.5
  79.7 0.7 bitcast_dynamic-update-slice_fusion.2
  80.3 0.3 convolution_bitcast_fusion.5
  80.7 0.7 bitcast_dynamic-update-slice_fusion.2
  81.4 0.3 convolution_bitcast_fusion.5
  81.8 0.7 bitcast_dynamic-update-slice_fusion.2
  82.5 0.3 convolution_bitcast_fusion.5
  82.9 0.7 bitcast_dynamic-update-slice_fusion.2
  83.5 0.3 convolution_bitcast_fusion.5
  83.9 0.7 bitcast_dynamic-update-slice_fusion.2
  84.6 0.3 convolution_bitcast_fusion.5
  85.0 0.7 bitcast_dynamic-update-slice_fusion.2
  85.7 0.3 convolution_bitcast_fusion.5
  86.1 0.7 bitcast_dynamic-update-slice_fusion.2
  86.7 0.3 convolution_bitcast_fusion.5
  87.1 0.7 bitcast_dynamic-update-slice_fusion.2
  87.8 0.3 convolution_bitcast_fusion.5
  88.2 0.7 bitcast_dynamic-update-slice_fusion.2
  88.9 0.3 convolution_bitcast_fusion.5
  89.3 0.7 bitcast_dynamic-update-slice_fusion.2
  89.9 0.3 convolution_bitcast_fusion.5
  90.3 0.7 bitcast_dynamic-update-slice_fusion.2
  91.0 0.3 convolution_bitcast_fusion.5
  91.4 4.1 %copy.16 = f32[64,4,16,128]{3,2,1,0:T(8,128)} copy(f32[64,4,16,128]{3,0,1,2:T(8,128)} %bitcast.53) | data formatting | bytes 4194304 | tf_op jit(solution)/shard_map/transpose | solution.py:87
  (68 shorter events, 0.7 us)
Async XLA Ops:
  5.1 6.5 %copy-start = (s32[4,1,2048]{2,1,0:T(1,128)S(1)}, s32[4,1,2048]{2,1,0:T(1,128)}, u32[]{:S(2)}) copy-start(s32[4,1,2048]{2,1,0:T(1,128)} %param.7) | copy-start | bytes 98308
  5.1 54.6 %all-to-all-start = ((f32[1,16,16,1,2048]{4,3,1,0,2:T(1,128)}), f32[1,16,16,1,2048]{4,3,1,0,2:T(1,128)S(1)}, u32[]{:S(2)}, u32[]{:S(2)}) async-start(f32[1,16,16,1,2048]{4,3,1,0,2:T(1,128)} %copy.10), calls=%async_computation | async-start | bytes 4194304 | tf_op jit(solution)/shard_map/all_to_all | solution.py:82
  68.4 5.9 %collective-permute-start = (f32[64,4,128]{2,0,1:T(8,128)S(1)}, f32[64,4,128]{2,0,1:T(8,128)S(1)}, u32[]{:S(2)}, u32[]{:S(2)}) collective-permute-start(f32[64,4,128]{2,0,1:T(8,128)S(1)} %get-tuple-element.74), channel_id=1, source_target_pairs={{0,2},{1,3},{4,6},{5,7},{8,10},{9,11},{12,14},{13,15},{16,18},{17,... | collective-permute-start | bytes 393224 | tf_op jit(solution)/shard_map/while/body/eval_jaxpr/ppermute | solution.py:12
where the time goes:
time: 95.8 us; the launch traced here: 95.5 us
  waiting for transfers between devices  50.6 us (53%)
  local copies, waits for them, and re-layouts  12.1 us (13%)
  matrix products  10.9 us (11%)
  other arithmetic  10.8 us (11%)
  starting transfers between devices  9.85 us (10%)
  loops' own time  1.22 us (1%)
    all_to_all x1, waiting for transfers between devices, local(): lax.all_to_all(runoff, 'basin', split_axis=2, concat_axis=1, tiled=True)  48.1 us
    dot_general x32, matrix products, advance(): jnp.einsum('mtj,tji->mti', summed, column_onehot(target_col, jnp.float32)...  10.9 us
    dynamic_update_slice x16, other arithmetic, sweep_tile(): lax.scan(advance, inflow, (jnp.moveaxis(water_cols, 2, 0), jnp.moveaxis(t...  10.7 us
    all_to_all x1, starting transfers between devices, local(): lax.all_to_all(runoff, 'basin', split_axis=2, concat_axis=1, tiled=True)  6.45 us
    unnamed x5, local copies, waits for them, and re-layouts  6.37 us
    transpose x1, local copies, waits for them, and re-layouts, local(): jnp.transpose(columns_out, (1, 2, 0, 3))  4.13 us
    ppermute x1, starting transfers between devices, from_behind(): return lax.ppermute(value, axis, pairs)  3.4 us
    ppermute x1, waiting for transfers between devices, from_behind(): return lax.ppermute(value, axis, pairs)  2.49 us
  transfers between devices with their start and end apart: 2, of which 2 were waited for; matrix products, arithmetic and copies ran while one was open for 0% of the time, Pallas kernels for 0%

commit v1 on v0

--- a/solution.py
+++ b/solution.py
@@ -2,6 +2,7 @@
 import jax.numpy as jnp
 from jax import lax
 from jax.sharding import PartitionSpec as P
+from jax.lax import all_to_all, axis_size
 
 ROWS = 128
 
@@ -79,7 +80,10 @@
 def local(runoff, directions):
     cell_count = runoff.shape[4]
     col_count = cell_count // ROWS
-    regrouped = lax.all_to_all(runoff, "basin", split_axis=2, concat_axis=1, tiled=True)
+    copies_deliver = lambda arr_in, row_axis: jnp.concatenate(
+        all_to_all(jnp.stack(jnp.split(arr_in, axis_size(row_axis), 2), 0), row_axis, 0, 0), 1
+    )
+    regrouped = copies_deliver(runoff, "basin")
     member_count, tile_count = (regrouped.shape[1], regrouped.shape[2])
     water_cols = regrouped.reshape(member_count, tile_count, col_count, ROWS)
     targets = target_rows(directions).reshape(tile_count, col_count, ROWS)

time: 95.8 us -> 130 us (1.36)
  matrix products: 10.9 us -> 40 us
  other arithmetic: 10.8 us -> 18.3 us
  local copies, waits for them, and re-layouts: 12.1 us -> 9.2 us
    dot_general x32, matrix products: 10.9 us -> 40 us  [advance(): jnp.einsum('mtj,tji->mti', summed, column_onehot(target_col, jnp.float32)...]
    unnamed x5 -> x2, local copies, waits for them, and re-layouts: 6.37 us -> 0.01 us
    dynamic_update_slice x16, other arithmetic: 10.7 us -> 14.9 us  [sweep_tile(): lax.scan(advance, inflow, (jnp.moveaxis(water_cols, 2, 0), jnp.moveaxis(t...]
    another operation x0 -> x1, local copies, waits for them, and re-layouts: none -> 3.44 us  [local(): jnp.stack(jnp.split(arr_in, axis_size(row_axis), 2), 0)]
    another operation x0 -> x1, other arithmetic: none -> 3.24 us  [local(): jnp.stack(jnp.split(arr_in, axis_size(row_axis), 2), 0)]
    while x2, local copies, waits for them, and re-layouts: 0.69 us -> 2.55 us  [sweep_tile(): lax.scan(advance, inflow, (jnp.moveaxis(water_cols, 2, 0), jnp.moveaxis(t...]
    transpose x1, local copies, waits for them, and re-layouts: 4.13 us -> 2.54 us  [local(): jnp.transpose(columns_out, (1, 2, 0, 3))]
where the time goes in v1:
time: 130 us; the launch traced here: 129 us
  waiting for transfers between devices  50.6 us (39%)
  matrix products  40 us (31%)
  other arithmetic  18.3 us (14%)
  starting transfers between devices  9.85 us (8%)
  local copies, waits for them, and re-layouts  9.2 us (7%)
    all_to_all x1, waiting for transfers between devices, local(): all_to_all(jnp.stack(jnp.split(arr_in, axis_size(row_axis), 2), 0), row_a...  48.1 us
    dot_general x32, matrix products, advance(): jnp.einsum('mtj,tji->mti', summed, column_onehot(target_col, jnp.float32)...  40 us
    dynamic_update_slice x16, other arithmetic, sweep_tile(): lax.scan(advance, inflow, (jnp.moveaxis(water_cols, 2, 0), jnp.moveaxis(t...  14.9 us
    all_to_all x1, starting transfers between devices, local(): all_to_all(jnp.stack(jnp.split(arr_in, axis_size(row_axis), 2), 0), row_a...  6.45 us
    another operation x1, local copies, waits for them, and re-layouts, local(): jnp.stack(jnp.split(arr_in, axis_size(row_axis), 2), 0)  3.44 us
    ppermute x1, starting transfers between devices, from_behind(): return lax.ppermute(value, axis, pairs)  3.4 us
    another operation x1, other arithmetic, local(): jnp.stack(jnp.split(arr_in, axis_size(row_axis), 2), 0)  3.24 us
  transfers between devices with their start and end apart: 2, of which 2 were waited for; matrix products, arithmetic and copies ran while one was open for 0% of the time, Pallas kernels for 0%

profile of v1, /device:TPU:0, one launch (start us, length us, event | category | flops | bytes accessed | tf_op | source)
XLA Modules:
  0.0 129.1 jit_solution(16076739067042900065)
XLA Ops:
  0.0 3.4 %slice_bitcast_fusion.3 = (f32[1,1,16,4,1,2048]{5,4,3,2,1,0:T(1,128)S(1)}, f32[1,1,16,4,1,2048]{5,4,3,2,1,0:T(1,128)S(1)}, f32[1,1,16,4,1,2048]{5,4,3,2,1,0:T(1,128)S(1)}, f32[1,1,16,4,1,2048]{5,4,3,2,1,0:T(1,128)S(1)}) fusion(f32[1,16,16,1,2048]{4,3,2,1,0:T(1,128)} %param.6), kind=kLoop, calls=%fused_computation.18 | loop fusion | bytes 4194304 | tf_op jit(solution)/shard_map/stack | solution.py:84
  3.5 3.2 %pad_maximum_fusion = f32[4,1,16,4,1,2048]{5,4,3,2,1,0:T(1,128)} fusion(f32[1,1,16,4,1,2048]{5,4,3,2,1,0:T(1,128)S(1)} %get-tuple-element.105, f32[1,1,16,4,1,2048]{5,4,3,2,1,0:T(1,128)S(1)} %get-tuple-element.106, f32[1,1,16,4,1,2048]{5,4,3,2,1,0:T(1,128)S(1)} %get-tuple-element.104, f32[1,1,16,4,1,2048]{5,4,3,2,1,0:T(1,128)S(1)} %get-tuple-element.103), kind=kLoop, calls=%fused_computation.14 | loop fusion | flops 1572864 | bytes 4194304 | tf_op jit(solution)/shard_map/stack | solution.py:84
  6.7 0.0 copy-start
  6.7 6.4 %all-to-all-start = ((f32[4,1,16,4,1,2048]{5,4,3,2,1,0:T(1,128)}), f32[4,1,16,4,1,2048]{5,4,3,2,1,0:T(1,128)S(1)}, u32[]{:S(2)}, u32[]{:S(2)}) async-start(f32[4,1,16,4,1,2048]{5,4,3,2,1,0:T(1,128)} %pad_maximum_fusion), calls=%async_computation | async-start | bytes 4194304 | tf_op jit(solution)/shard_map/all_to_all | solution.py:84
  13.2 0.0 copy-done
  13.2 0.1 fusion.6
  13.3 48.1 %all-to-all-done = f32[4,1,16,4,1,2048]{5,4,3,2,1,0:T(1,128)S(1)} async-done(((f32[4,1,16,4,1,2048]{5,4,3,2,1,0:T(1,128)}), f32[4,1,16,4,1,2048]{5,4,3,2,1,0:T(1,128)S(1)}, u32[]{:S(2)}, u32[]{:S(2)}) %all-to-all-start) | async-done | bytes 2097184 | tf_op jit(solution)/shard_map/all_to_all | solution.py:84
  61.3 2.5 %copy.6 = f32[16,64,4,128]{3,1,2,0:T(8,128)} copy(f32[16,64,4,128]{3,0,2,1:T(8,128)S(1)} %bitcast.52) | data formatting | bytes 4194304 | tf_op jit(solution)/shard_map/while | solution.py:41
  63.9 20.9 %while.4 = (s32[]{:T(128)}, f32[64,4,128]{2,0,1:T(8,128)S(1)}, s32[16,4,128]{2,1,0:T(4,128)S(1)}, f32[16,64,4,128]{3,1,2,0:T(8,128)}, s32[]{:T(128)}) while((s32[]{:T(128)}, f32[64,4,128]{2,0,1:T(8,128)S(1)}, s32[16,4,128]{2,1,0:T(4,128)S(1)}, f32[16,64,4,128]{3,1,2,0:T(8,128)}, s32[]{:T(128)}) %tuple.39), condition=%wide.region_1.2_spmd, body=%wide.region_0.1_spmd.sunk | while | flops 50429952 | bytes 661581 | solution.py:41
  63.9 1.2 convolution_bitcast_fusion.4
  65.2 1.2 convolution_bitcast_fusion.4
  66.6 1.2 convolution_bitcast_fusion.4
  67.9 1.2 convolution_bitcast_fusion.4
  69.2 1.2 convolution_bitcast_fusion.4
  70.5 1.2 convolution_bitcast_fusion.4
  71.8 1.2 convolution_bitcast_fusion.4
  73.1 1.2 convolution_bitcast_fusion.4
  74.4 1.2 convolution_bitcast_fusion.4
  75.7 1.2 convolution_bitcast_fusion.4
  77.0 1.2 convolution_bitcast_fusion.4
  78.3 1.2 convolution_bitcast_fusion.4
  79.6 1.2 convolution_bitcast_fusion.4
  81.0 1.2 convolution_bitcast_fusion.4
  82.3 1.2 convolution_bitcast_fusion.4
  83.6 1.2 convolution_bitcast_fusion.4
  84.8 3.4 %collective-permute-start = (f32[64,4,128]{2,0,1:T(8,128)S(1)}, f32[64,4,128]{2,0,1:T(8,128)S(1)}, u32[]{:S(2)}, u32[]{:S(2)}) collective-permute-start(f32[64,4,128]{2,0,1:T(8,128)S(1)} %get-tuple-element.74), channel_id=1, source_target_pairs={{0,2},{1,3},{4,6},{5,7},{8,10},{9,11},{12,14},{13,15},{16,18},{17,... | collective-permute-start | bytes 393224 | tf_op jit(solution)/shard_map/while/body/eval_jaxpr/ppermute | solution.py:13
  88.3 2.5 %collective-permute-done = f32[64,4,128]{2,0,1:T(8,128)S(1)} collective-permute-done((f32[64,4,128]{2,0,1:T(8,128)S(1)}, f32[64,4,128]{2,0,1:T(8,128)S(1)}, u32[]{:S(2)}, u32[]{:S(2)}) %collective-permute-start) | collective-permute-done | bytes 131104 | tf_op jit(solution)/shard_map/while/body/eval_jaxpr/ppermute | solution.py:13
  90.7 35.8 %while.5 = (s32[]{:T(128)}, f32[64,4,128]{2,0,1:T(8,128)S(1)}, f32[16,64,4,128]{3,1,2,0:T(8,128)S(1)}, s32[16,4,128]{2,1,0:T(4,128)S(1)}, f32[16,64,4,128]{3,1,2,0:T(8,128)}, /*index=5*/s32[]{:T(128)}) while((s32[]{:T(128)}, f32[64,4,128]{2,0,1:T(8,128)S(1)}, f32[16,64,4,128]{3,1,2,0:T(8,128)S(1)}, s32[16,4,128]{2,1,0:T(4,128)S(1)}, ...), condition=%wide.region_3.4_spmd, body=%wide.region_2.3_spmd.sunk | while | flops 50462720 | bytes 1054809 | solution.py:41
  90.8 0.9 bitcast_dynamic-update-slice_fusion.2
  91.7 1.2 convolution_bitcast_fusion.5
  93.0 0.9 bitcast_dynamic-update-slice_fusion.2
  93.9 1.2 convolution_bitcast_fusion.5
  95.3 0.9 bitcast_dynamic-update-slice_fusion.2
  96.2 1.2 convolution_bitcast_fusion.5
  97.5 0.9 bitcast_dynamic-update-slice_fusion.2
  98.4 1.2 convolution_bitcast_fusion.5
  99.7 0.9 bitcast_dynamic-update-slice_fusion.2
  100.7 1.2 convolution_bitcast_fusion.5
  102.0 0.9 bitcast_dynamic-update-slice_fusion.2
  102.9 1.2 convolution_bitcast_fusion.5
  104.2 0.9 bitcast_dynamic-update-slice_fusion.2
  105.2 1.2 convolution_bitcast_fusion.5
  106.5 0.9 bitcast_dynamic-update-slice_fusion.2
  107.4 1.2 convolution_bitcast_fusion.5
  108.7 0.9 bitcast_dynamic-update-slice_fusion.2
  109.6 1.2 convolution_bitcast_fusion.5
  110.9 0.9 bitcast_dynamic-update-slice_fusion.2
  111.9 1.2 convolution_bitcast_fusion.5
  113.2 0.9 bitcast_dynamic-update-slice_fusion.2
  114.1 1.2 convolution_bitcast_fusion.5
  115.4 0.9 bitcast_dynamic-update-slice_fusion.2
  116.4 1.2 convolution_bitcast_fusion.5
  117.7 0.9 bitcast_dynamic-update-slice_fusion.2
  118.6 1.2 convolution_bitcast_fusion.5
  119.9 0.9 bitcast_dynamic-update-slice_fusion.2
  120.8 1.2 convolution_bitcast_fusion.5
  122.1 0.9 bitcast_dynamic-update-slice_fusion.2
  123.1 1.2 convolution_bitcast_fusion.5
  124.4 0.9 bitcast_dynamic-update-slice_fusion.2
  125.3 1.2 convolution_bitcast_fusion.5
  126.6 2.5 %copy.9 = f32[64,4,16,128]{3,2,1,0:T(8,128)} copy(f32[64,4,16,128]{3,0,1,2:T(8,128)S(1)} %bitcast.53) | data formatting | bytes 4194304 | tf_op jit(solution)/shard_map/transpose | solution.py:91
  (68 shorter events, 0.7 us)
Async XLA Ops:
  6.7 6.5 %copy-start = (s32[4,1,2048]{2,1,0:T(1,128)S(1)}, s32[4,1,2048]{2,1,0:T(1,128)}, u32[]{:S(2)}) copy-start(s32[4,1,2048]{2,1,0:T(1,128)} %param.7) | copy-start | bytes 98308
  6.7 54.6 %all-to-all-start = ((f32[4,1,16,4,1,2048]{5,4,3,2,1,0:T(1,128)}), f32[4,1,16,4,1,2048]{5,4,3,2,1,0:T(1,128)S(1)}, u32[]{:S(2)}, u32[]{:S(2)}) async-start(f32[4,1,16,4,1,2048]{5,4,3,2,1,0:T(1,128)} %pad_maximum_fusion), calls=%async_computation | async-start | bytes 4194304 | tf_op jit(solution)/shard_map/all_to_all | solution.py:84
  84.8 5.9 %collective-permute-start = (f32[64,4,128]{2,0,1:T(8,128)S(1)}, f32[64,4,128]{2,0,1:T(8,128)S(1)}, u32[]{:S(2)}, u32[]{:S(2)}) collective-permute-start(f32[64,4,128]{2,0,1:T(8,128)S(1)} %get-tuple-element.74), channel_id=1, source_target_pairs={{0,2},{1,3},{4,6},{5,7},{8,10},{9,11},{12,14},{13,15},{16,18},{17,... | collective-permute-start | bytes 393224 | tf_op jit(solution)/shard_map/while/body/eval_jaxpr/ppermute | solution.py:13
